TPU v7x, 32 devices: a whole 2x2x4 slice. The times are simulated.
32 devices in a mesh: dp: 8 (over z, y), mp: 4 (over x, core).
Axes of the slice: x: 2, y: 2, z: 4, core: 2. Of those that a mesh axis runs over, the one named last changes fastest.
Arguments:
- latents: bfloat16 [262144, 256], P(('dp', 'mp')), may hold values from -6 to 6
- proj_weight: bfloat16 [18, 256], replicated, may hold values from -0.375 to 0.375
- proj_bias: float32 [18], replicated, may hold values from -2.5 to 2.5
- fill: int32 [2048], replicated, may hold values from 0 to 128, as said below
- target: int32 [2048], replicated, may hold values from -1 to 7, as said below
- target_slot: int32 [2048], replicated, may hold values from -1 to 31, as said below
Outputs:
- latent_grad: bfloat16 [131072, 256], P(('dp', 'mp'))
- weight_grad: float32 [18, 256], replicated
- entropy_loss: float32 [], replicated
Inputs may be any that keep to these rules, and one draw needn't show every extreme that they name: `fill`: zero exactly on the empty slots of a device, which are those whose target is -1. `target`: blocks go to devices with the same mp index. Each device receives exactly 32 blocks, one in each of its positions; at most 8 blocks goes from one device to any one index of dp, and some device does send 8 block to an index. -1 marks an empty slot. `target_slot`: -1 exactly where target is -1.
All inputs are finite; a program needn't handle non-finite values.
Results may differ from a plain program's by a relative error of at most 0.0049.
Values may be sent and summed in bfloat16 or wider, within the bound.
A program may use at most 64 MiB of HBM per device.

v0:
```python
import jax
import jax.numpy as jnp
from jax import lax
from jax.sharding import PartitionSpec as P

BLK = 128
OUT_SLOTS = 32
sharpness = 2.0


def routing(fill, target, target_slot, n_dp, n_mp, in_slots, capacity, own_dp, own_mp):
    col_shape = (n_dp, n_mp, in_slots)
    col_fill = lax.dynamic_index_in_dim(fill.reshape(col_shape), own_mp, 1, keepdims=False)
    col_target = lax.dynamic_index_in_dim(target.reshape(col_shape), own_mp, 1, keepdims=False)
    col_slot = lax.dynamic_index_in_dim(target_slot.reshape(col_shape), own_mp, 1, keepdims=False)
    matches = col_target[:, :, None] == col_target[:, None, :]
    earlier = lax.broadcasted_iota(jnp.int32, (in_slots, in_slots), 0) < lax.broadcasted_iota(
        jnp.int32, (in_slots, in_slots), 1
    )
    arrival_rank = jnp.sum((matches & earlier[None]).astype(jnp.int32), axis=1)
    sources = lax.broadcasted_iota(jnp.int32, (n_dp, in_slots), 0)
    arrive = sources * capacity + arrival_rank
    own_target = lax.dynamic_index_in_dim(col_target, own_dp, 0, keepdims=False)
    own_rank = lax.dynamic_index_in_dim(arrival_rank, own_dp, 0, keepdims=False)
    send_slot = jnp.where(own_target >= 0, own_target * capacity + own_rank, n_dp * capacity)
    chosen = (
        jnp.full((n_dp * capacity,), in_slots, jnp.int32)
        .at[send_slot]
        .set(jnp.arange(in_slots, dtype=jnp.int32), mode="drop")
    )
    landing = jnp.where(col_target == own_dp, col_slot, OUT_SLOTS).reshape(-1)
    gather_order = (
        jnp.zeros((OUT_SLOTS,), jnp.int32).at[landing].set(arrive.reshape(-1), mode="drop")
    )
    out_fill = jnp.zeros((OUT_SLOTS,), jnp.int32).at[landing].set(col_fill.reshape(-1), mode="drop")
    own_fill = lax.dynamic_index_in_dim(col_fill, own_dp, 0, keepdims=False)
    return (chosen, gather_order, out_fill, own_fill)


def statistics(blocks, fills, proj_weight, proj_bias):
    logits = (
        jnp.einsum("nkd,bd->nbk", blocks, proj_weight, preferred_element_type=jnp.float32)
        + proj_bias[None, :, None]
    )
    scaled = sharpness * logits
    token_mask = (lax.broadcasted_iota(jnp.int32, (1, 1, BLK), 2) < fills[:, None, None]).astype(
        jnp.float32
    )
    probability = jax.nn.sigmoid(scaled)
    entropy = jax.nn.softplus(scaled) - probability * scaled
    bit_sums = jnp.sum(probability * token_mask, axis=(0, 2))
    entropy_sum = jnp.sum(entropy * token_mask)
    variance = probability * (1.0 - probability) * token_mask
    return (bit_sums, entropy_sum, -2.0 * scaled * variance, 2.0 * variance)


def local(latents, proj_weight, proj_bias, fill, target, target_slot):
    n_dp = lax.axis_size("dp")
    n_mp = lax.axis_size("mp")
    own_dp = lax.axis_index("dp")
    own_mp = lax.axis_index("mp")
    feature_width = latents.shape[1]
    in_slots = latents.shape[0] // BLK
    capacity = max(1, 2 * OUT_SLOTS // n_dp)
    chosen, gather_order, out_fill, own_fill = routing(
        fill, target, target_slot, n_dp, n_mp, in_slots, capacity, own_dp, own_mp
    )
    token_count = jnp.sum(fill).astype(jnp.float32)
    loaded = latents.reshape(in_slots, BLK, feature_width)
    bit_sums, entropy_sum, first_term, second_term = statistics(
        loaded, own_fill, proj_weight, proj_bias
    )
    first_rounded = first_term.astype(jnp.bfloat16)
    second_rounded = second_term.astype(jnp.bfloat16)
    first_weight = jnp.einsum(
        "nbk,nkd->bd", first_rounded, loaded, preferred_element_type=jnp.float32
    )
    second_weight = jnp.einsum(
        "nbk,nkd->bd", second_rounded, loaded, preferred_element_type=jnp.float32
    )
    bit_sums, entropy_sum = lax.psum((bit_sums, entropy_sum), ("dp", "mp"))
    marginal = bit_sums / token_count
    codebook = -jnp.sum(marginal * jnp.log(marginal) + (1.0 - marginal) * jnp.log(1.0 - marginal))
    entropy_loss = entropy_sum / token_count - codebook
    log_odds = jnp.log(1.0 - marginal) - jnp.log(marginal)
    cotangent = (first_term - second_term * log_odds[None, :, None]).astype(jnp.bfloat16)
    padded_cot = jnp.concatenate(
        [cotangent, jnp.zeros((1,) + cotangent.shape[1:], cotangent.dtype)]
    )
    outgoing_cot = padded_cot[chosen].reshape(n_dp * capacity * cotangent.shape[1], BLK)
    arrived_cot = lax.all_to_all(outgoing_cot, "dp", split_axis=0, concat_axis=0, tiled=True)
    landed = arrived_cot.reshape(n_dp * capacity, cotangent.shape[1], BLK)[gather_order]
    latent_grad = jnp.einsum(
        "nbk,bd->nkd", landed, proj_weight, preferred_element_type=jnp.float32
    ).astype(jnp.bfloat16)
    first_weight, second_weight = lax.psum((first_weight, second_weight), ("dp", "mp"))
    weight_grad = (first_weight - second_weight * log_odds[:, None]) / jnp.sqrt(token_count)
    return (latent_grad.reshape(-1, feature_width), weight_grad, entropy_loss)


def solution(mesh):
    placed = (P(("dp", "mp"), None), P(), P(), P(), P(), P())
    return jax.shard_map(
        local,
        mesh=mesh,
        in_specs=placed,
        out_specs=(P(("dp", "mp"), None), P(), P()),
        check_vma=False,
    )
```

profile of v0, /device:TPU:0, one launch (start us, length us, event | category | flops | bytes accessed | tf_op | source)
XLA Modules:
  0.0 73.5 jit_solution(14534599684617418197)
XLA Ops:
  0.6 0.0 copy-start
  0.7 0.8 %reshape.158 = s32[8,4,64]{2,1,0:T(4,128)S(1)} reshape(s32[2048]{0:T(1024)} %param.9) | data formatting | bytes 16384 | tf_op jit(solution)/shard_map/reshape | solution.py:13
  1.4 1.3 %reduce_sum.46 = s32[]{:T(128)} reduce(s32[2048]{0:T(1024)} %param.9, s32[]{:T(128)} %constant.78.clone.1), dimensions={0}, to_apply=%region_2.3 | reduce | flops 2047 | bytes 8200 | tf_op jit(solution)/shard_map/reduce_sum | solution.py:68
  2.8 0.1 fusion.19
  2.9 0.0 copy-done
  2.9 0.0 copy-start.3
  2.9 4.2 %fusion.3 = (f32[]{:T(128)}, f32[18]{0:T(128)S(1)}, f32[18,64,128]{2,0,1:T(8,128)S(1)}) fusion(f32[64,128]{1,0:T(8,128)S(1)} %fusion.19, f32[18]{0:T(128)} %param.8, bf16[64,128,256]{2,1,0:T(8,128)(2,1)} %bitcast.89, bf16[18,256]{1,0:T(8,128)(2,1)S(1)} %copy-done), kind=kOutput, calls=%fused_computation.13 | convolution fusion | flops 78004208 | bytes 4826260 | tf_op jit(solution)/shard_map/nkd,bd->nbk/dot_general | solution.py:42
  7.1 0.0 copy-done.3
  7.1 0.8 %convolution_bitcast_fusion.1 = f32[18,256]{1,0:T(8,128)S(1)} fusion(bf16[64,128,256]{2,1,0:T(8,128)(2,1)S(1)} %bitcast.90, f32[18,64,128]{2,0,1:T(8,128)S(1)} %get-tuple-element.15, f32[64,128]{1,0:T(8,128)S(1)} %fusion.19), kind=kOutput, calls=%fused_computation.9 | convolution fusion | flops 76972032 | bytes 4835328 | tf_op jit(solution)/shard_map/nbk,nkd->bd/dot_general | solution.py:75
  7.9 0.0 copy-start.2
  7.9 0.8 %convolution_bitcast_fusion = f32[18,256]{1,0:T(8,128)S(1)} fusion(bf16[64,128,256]{2,1,0:T(8,128)(2,1)S(1)} %bitcast.91, f32[64,128]{1,0:T(8,128)S(1)} %fusion.19, f32[18,64,128]{2,0,1:T(8,128)S(1)} %get-tuple-element.15), kind=kOutput, calls=%fused_computation.8 | convolution fusion | flops 76824576 | bytes 4835328 | tf_op jit(solution)/shard_map/nbk,nkd->bd/dot_general | solution.py:78
  9.4 0.0 copy-done.1
  9.4 0.1 reshape.159
  9.5 0.0 copy-done.2
  9.5 0.1 reshape.161
  9.6 0.1 convert_reduce_fusion
  9.7 0.8 %scatter_custom_fusion = s32[64]{0:T(128)S(1)} fusion(s32[64]{0:T(128)S(1)} %fusion.27, s32[64]{0:T(128)S(1)} %iota.34, s32[]{:T(128)} %constant.88.clone.1), kind=kCustom, calls=%fused_computation.69 | custom fusion | bytes 260 | tf_op jit(solution)/shard_map/scatter | solution.py:29
  10.6 42.8 %all-reduce.1 = (f32[18]{0:T(128)S(1)}, f32[18,256]{1,0:T(8,128)S(1)}, f32[18,256]{1,0:T(8,128)S(1)}, f32[]{:T(128)}) all-reduce(f32[18]{0:T(128)S(1)} %get-tuple-element.4, f32[18,256]{1,0:T(8,128)S(1)} %convolution_bitcast_fusion.1, f32[18,256]{1,0:T(8,128)S(1)} %convolution_bitcast_fusion, ...), channel_id=1, replica_groups=mesh['dp'=8,'mp'=4] {'dp','mp'}, use_global_device_ids=true, to_apply=%region_1.2 | all-reduce | flops 9235 | bytes 73880 | tf_op jit(solution)/shard_map/psum | solution.py:81
  53.3 0.6 fusion.28
  53.9 0.4 subtract_convert_fusion
  54.4 0.7 gather_fusion
  55.0 0.8 %all_to_all.6 = bf16[8,144,128]{2,1,0:T(8,128)(2,1)} reshape(bf16[64,18,128]{2,1,0:T(8,128)(2,1)S(1)} %gather_fusion) | data formatting | bytes 589824 | tf_op jit(solution)/shard_map/all_to_all | solution.py:91
  55.8 5.3 %all-to-all-start = ((bf16[8,144,128]{2,1,0:T(8,128)(2,1)}), bf16[8,144,128]{2,1,0:T(8,128)(2,1)S(1)}, u32[]{:S(2)}, u32[]{:S(2)}) async-start(bf16[8,144,128]{2,1,0:T(8,128)(2,1)} %all_to_all.6), calls=%async_computation | async-start | bytes 589824 | tf_op jit(solution)/shard_map/all_to_all | solution.py:91
  61.2 0.1 select_n.80
  61.3 0.1 broadcast_add_fusion
  61.3 0.1 reshape.191
  62.7 2.4 %scatter_custom_fusion.1 = s32[32]{0:T(128)S(1)} fusion(s32[512]{0:T(512)S(1)} %bitcast.88, s32[512]{0:T(512)S(1)} %reshape.191, s32[]{:T(128)} %constant.78.clone.1), kind=kCustom, calls=%fused_computation.67 | custom fusion | bytes 132 | tf_op jit(solution)/shard_map/scatter | solution.py:33
  65.2 0.7 subtract_divide_fusion
  65.9 3.7 %all-to-all-done = bf16[8,144,128]{2,1,0:T(8,128)(2,1)S(1)} async-done(((bf16[8,144,128]{2,1,0:T(8,128)(2,1)}), bf16[8,144,128]{2,1,0:T(8,128)(2,1)S(1)}, u32[]{:S(2)}, u32[]{:S(2)}) %all-to-all-start) | async-done | bytes 294944 | tf_op jit(solution)/shard_map/all_to_all | solution.py:91
  69.6 0.1 reshape.160
  69.7 0.6 gather_fusion.1
  70.3 2.1 %convolution_convert_fusion = bf16[32,128,256]{2,1,0:T(8,128)(2,1)} fusion(bf16[32,18,128]{2,1,0:T(8,128)(2,1)S(1)} %gather_fusion.1, bf16[18,256]{1,0:T(8,128)(2,1)S(1)} %copy-done), kind=kOutput, calls=%fused_computation.5 | convolution fusion | flops 38797312 | bytes 2253824 | tf_op jit(solution)/shard_map/nbk,bd->nkd/dot_general | solution.py:93
  (14 shorter events, 0.1 us)
Async XLA Ops:
  0.6 2.2 %copy-start = (bf16[18,256]{1,0:T(8,128)(2,1)S(1)}, bf16[18,256]{1,0:T(8,128)(2,1)}, u32[]{:S(2)}) copy-start(bf16[18,256]{1,0:T(8,128)(2,1)} %param.7) | copy-start | bytes 27652
  2.9 4.2 %copy-start.3 = (bf16[8192,256]{1,0:T(8,128)(2,1)S(1)}, bf16[8192,256]{1,0:T(8,128)(2,1)}, u32[]{:S(2)}) copy-start(bf16[8192,256]{1,0:T(8,128)(2,1)} %param.6) | copy-start | bytes 12582916
  7.9 1.5 %copy-start.1 = (s32[2048]{0:T(1024)S(1)}, s32[2048]{0:T(1024)}, u32[]{:S(2)}) copy-start(s32[2048]{0:T(1024)} %param.10) | copy-start | bytes 24580
  7.9 1.5 %copy-start.2 = (s32[2048]{0:T(1024)S(1)}, s32[2048]{0:T(1024)}, u32[]{:S(2)}) copy-start(s32[2048]{0:T(1024)} %param.11) | copy-start | bytes 24580
  55.8 13.7 %all-to-all-start = ((bf16[8,144,128]{2,1,0:T(8,128)(2,1)}), bf16[8,144,128]{2,1,0:T(8,128)(2,1)S(1)}, u32[]{:S(2)}, u32[]{:S(2)}) async-start(bf16[8,144,128]{2,1,0:T(8,128)(2,1)} %all_to_all.6), calls=%async_computation | async-start | bytes 589824 | tf_op jit(solution)/shard_map/all_to_all | solution.py:91
where the time goes:
time: 74 us; the launch traced here: 73.5 us
  blocking collectives  42.8 us (58%)
  matrix products  7.88 us (11%)
  local copies, waits for them, and re-layouts  6.53 us (9%)
  starting transfers between devices  5.3 us (7%)
  between operations  3.96 us (5%)
  waiting for transfers between devices  3.68 us (5%)
  other arithmetic  3.36 us (5%)
    psum x1, blocking collectives, local(): bit_sums, entropy_sum = lax.psum((bit_sums, entropy_sum), ('dp', 'mp'))  42.8 us
    all_to_all x1, starting transfers between devices, local(): lax.all_to_all(outgoing_cot, 'dp', split_axis=0, concat_axis=0, tiled=True)  5.3 us
    dot_general x1, matrix products, statistics(): jnp.einsum('nkd,bd->nbk', blocks, proj_weight, preferred_element_type=jnp...  4.21 us
    all_to_all x1, waiting for transfers between devices, local(): lax.all_to_all(outgoing_cot, 'dp', split_axis=0, concat_axis=0, tiled=True)  3.68 us
    scatter x1, local copies, waits for them, and re-layouts, routing(): jnp.zeros((OUT_SLOTS,), jnp.int32).at[landing]  2.44 us
    dot_general x1, matrix products, local(): jnp.einsum('nbk,bd->nkd', landed, proj_weight, preferred_element_type=jnp...  2.08 us
  transfers between devices with their start and end apart: 1, of which 1 were waited for; matrix products, arithmetic and copies ran while one was open for 5% of the time, Pallas kernels for 0%

commit v1 on v0

--- a/solution.py
+++ b/solution.py
@@ -78,7 +78,7 @@
     second_weight = jnp.einsum(
         "nbk,nkd->bd", second_rounded, loaded, preferred_element_type=jnp.float32
     )
-    bit_sums, entropy_sum = lax.psum((bit_sums, entropy_sum), ("dp", "mp"))
+    bit_sums, entropy_sum = lax.psum(lax.psum((bit_sums, entropy_sum), "mp"), "dp")
     marginal = bit_sums / token_count
     codebook = -jnp.sum(marginal * jnp.log(marginal) + (1.0 - marginal) * jnp.log(1.0 - marginal))
     entropy_loss = entropy_sum / token_count - codebook

time: 74 us -> 101 us (1.36)
  blocking collectives: 42.8 us -> 71.6 us
  waiting for transfers between devices: 3.68 us -> 0.01 us
  matrix products: 7.88 us -> 10 us
  starting transfers between devices: 5.3 us -> 3.42 us
  local copies, waits for them, and re-layouts: 6.53 us -> 8.21 us
    psum x1 -> x3, blocking collectives: 42.8 us -> 71.6 us  [the longest x1 40.3 us: local(): lax.psum((first_weight, second_weight), ('dp', 'mp'))]
    all_to_all x1, waiting for transfers between devices: 3.68 us -> 0.01 us  [local(): lax.all_to_all(outgoing_cot, 'dp', split_axis=0, concat_axis=0, tiled=True)]
    dot_general x1, matrix products: 0.82 us -> 3.13 us  [local(): jnp.einsum('nbk,nkd->bd', first_rounded, loaded, preferred_element_type=j...]
    all_to_all x1, starting transfers between devices: 5.3 us -> 3.42 us  [local(): lax.all_to_all(outgoing_cot, 'dp', split_axis=0, concat_axis=0, tiled=True)]
  transfers between devices with their start and end apart: 1 -> 1, of which waited for: 1 -> 0; matrix products, arithmetic and copies ran while one was open for 5% -> 7% of each run, Pallas kernels for 0% -> 0%
where the time goes in v1:
time: 101 us
  blocking collectives  71.6 us (71%)
  matrix products  10 us (10%)
  local copies, waits for them, and re-layouts  8.21 us (8%)
  between operations  3.95 us (4%)
  starting transfers between devices  3.42 us (3%)
  other arithmetic  3.36 us (3%)
    psum x1, blocking collectives, local(): lax.psum((first_weight, second_weight), ('dp', 'mp'))  40.3 us
    psum x1, blocking collectives, local(): lax.psum(lax.psum((bit_sums, entropy_sum), 'mp'), 'dp')  22.3 us
    psum x1, blocking collectives, local(): lax.psum((bit_sums, entropy_sum), 'mp')  8.97 us
    dot_general x1, matrix products, statistics(): jnp.einsum('nkd,bd->nbk', blocks, proj_weight, preferred_element_type=jnp...  4.06 us
    all_to_all x1, starting transfers between devices, local(): lax.all_to_all(outgoing_cot, 'dp', split_axis=0, concat_axis=0, tiled=True)  3.42 us
    dot_general x1, matrix products, local(): jnp.einsum('nbk,nkd->bd', first_rounded, loaded, preferred_element_type=j...  3.13 us
    scatter x1, local copies, waits for them, and re-layouts, routing(): jnp.zeros((OUT_SLOTS,), jnp.int32).at[landing]  2.44 us
    dot_general x1, matrix products, local(): jnp.einsum('nbk,bd->nkd', landed, proj_weight, preferred_element_type=jnp...  2.08 us
  transfers between devices with their start and end apart: 1, of which 0 were waited for; matrix products, arithmetic and copies ran while one was open for 7% of the time, Pallas kernels for 0%

profile of v1, /device:TPU:0, one launch (start us, length us, event | category | flops | bytes accessed | tf_op | source)
XLA Modules:
  0.0 100.5 jit_solution(7203812652973662267)
XLA Ops:
  0.6 0.0 copy-start
  0.7 0.8 reshape.158
  1.4 1.3 %reduce_sum.46 = s32[]{:T(128)} reduce(s32[2048]{0:T(1024)} %param.9, s32[]{:T(128)} %constant.78.clone.1), dimensions={0}, to_apply=%region_3.4 | reduce | flops 2047 | bytes 8200 | tf_op jit(solution)/shard_map/reduce_sum | solution.py:68
  3.4 0.8 reshape.159
  4.2 0.8 reshape.161
  5.0 0.1 convert_reduce_fusion
  5.2 0.8 scatter_custom_fusion
  6.0 0.1 fusion.19
  6.1 0.0 copy-done
  6.1 4.1 %fusion.3 = (f32[]{:T(128)}, f32[18]{0:T(128)S(1)}, f32[18,64,128]{2,0,1:T(8,128)S(1)}) fusion(f32[64,128]{1,0:T(8,128)S(1)} %fusion.19, f32[18]{0:T(128)} %param.8, bf16[64,128,256]{2,1,0:T(8,128)(2,1)} %bitcast.89, bf16[18,256]{1,0:T(8,128)(2,1)S(1)} %copy-done), kind=kOutput, calls=%fused_computation.13 | convolution fusion | flops 78004208 | bytes 4826260 | tf_op jit(solution)/shard_map/nkd,bd->nbk/dot_general | solution.py:42
  10.2 9.0 %all-reduce.3 = (f32[18]{0:T(128)S(1)}, f32[]{:T(128)}) all-reduce(f32[18]{0:T(128)S(1)} %get-tuple-element.4, f32[]{:T(128)} %get-tuple-element.3), channel_id=1, replica_groups=mesh['dp'=8,'mp'=4] {'mp'}, use_global_device_ids=true, to_apply=%region_1.2 | all-reduce | flops 19 | bytes 152 | tf_op jit(solution)/shard_map/psum | solution.py:81
  19.1 22.3 %all-reduce.2 = (f32[18]{0:T(128)S(1)}, f32[]{:T(128)}) all-reduce(f32[18]{0:T(128)S(1)} %get-tuple-element.9, f32[]{:T(128)} %get-tuple-element.10), channel_id=1, replica_groups=mesh['dp'=8,'mp'=4] {'dp'}, use_global_device_ids=true, to_apply=%region_2.3 | all-reduce | flops 19 | bytes 152 | tf_op jit(solution)/shard_map/psum | solution.py:81
  41.4 0.6 fusion.28
  42.1 0.3 subtract_convert_fusion
  42.5 0.7 gather_fusion
  43.1 0.8 all_to_all.6
  43.9 3.4 %all-to-all-start = ((bf16[8,144,128]{2,1,0:T(8,128)(2,1)}), bf16[8,144,128]{2,1,0:T(8,128)(2,1)S(1)}, u32[]{:S(2)}, u32[]{:S(2)}) async-start(bf16[8,144,128]{2,1,0:T(8,128)(2,1)} %all_to_all.6), calls=%async_computation | async-start | bytes 589824 | tf_op jit(solution)/shard_map/all_to_all | solution.py:91
  47.4 0.0 copy-start.1
  47.4 3.1 %convolution_bitcast_fusion.1 = f32[18,256]{1,0:T(8,128)S(1)} fusion(bf16[64,128,256]{2,1,0:T(8,128)(2,1)} %bitcast.90, f32[18,64,128]{2,0,1:T(8,128)S(1)} %get-tuple-element.17, f32[64,128]{1,0:T(8,128)S(1)} %fusion.19), kind=kOutput, calls=%fused_computation.9 | convolution fusion | flops 76972032 | bytes 4835328 | tf_op jit(solution)/shard_map/nbk,nkd->bd/dot_general | solution.py:75
  50.6 0.3 copy-done.1
  50.9 0.7 convolution_bitcast_fusion
  51.6 0.1 select_n.80
  51.7 0.1 broadcast_add_fusion
  51.8 0.1 reshape.191
  53.2 2.4 %scatter_custom_fusion.1 = s32[32]{0:T(128)S(1)} fusion(s32[512]{0:T(512)S(1)} %bitcast.88, s32[512]{0:T(512)S(1)} %reshape.191, s32[]{:T(128)} %constant.78.clone.1), kind=kCustom, calls=%fused_computation.67 | custom fusion | bytes 132 | tf_op jit(solution)/shard_map/scatter | solution.py:33
  55.6 40.3 %all-reduce.1 = (f32[18,256]{1,0:T(8,128)S(1)}, f32[18,256]{1,0:T(8,128)S(1)}) all-reduce(f32[18,256]{1,0:T(8,128)S(1)} %convolution_bitcast_fusion.1, f32[18,256]{1,0:T(8,128)S(1)} %convolution_bitcast_fusion), channel_id=1, replica_groups=mesh['dp'=8,'mp'=4] {'dp','mp'}, use_global_device_ids=true, to_apply=%region_7.8 | all-reduce | flops 9216 | bytes 73728 | tf_op jit(solution)/shard_map/psum | solution.py:96
  95.9 0.7 subtract_divide_fusion
  96.6 0.0 all-to-all-done
  96.6 0.1 reshape.160
  96.7 0.6 gather_fusion.1
  97.3 2.1 %convolution_convert_fusion = bf16[32,128,256]{2,1,0:T(8,128)(2,1)} fusion(bf16[32,18,128]{2,1,0:T(8,128)(2,1)S(1)} %gather_fusion.1, bf16[18,256]{1,0:T(8,128)(2,1)S(1)} %copy-done), kind=kOutput, calls=%fused_computation.5 | convolution fusion | flops 38797312 | bytes 2253824 | tf_op jit(solution)/shard_map/nbk,bd->nkd/dot_general | solution.py:93
  (13 shorter events, 0.2 us)
Async XLA Ops:
  0.6 5.5 %copy-start = (bf16[18,256]{1,0:T(8,128)(2,1)S(1)}, bf16[18,256]{1,0:T(8,128)(2,1)}, u32[]{:S(2)}) copy-start(bf16[18,256]{1,0:T(8,128)(2,1)} %param.7) | copy-start | bytes 27652
  43.9 52.7 %all-to-all-start = ((bf16[8,144,128]{2,1,0:T(8,128)(2,1)}), bf16[8,144,128]{2,1,0:T(8,128)(2,1)S(1)}, u32[]{:S(2)}, u32[]{:S(2)}) async-start(bf16[8,144,128]{2,1,0:T(8,128)(2,1)} %all_to_all.6), calls=%async_computation | async-start | bytes 589824 | tf_op jit(solution)/shard_map/all_to_all | solution.py:91
  47.4 3.5 %copy-start.1 = (bf16[8192,256]{1,0:T(8,128)(2,1)S(1)}, bf16[8192,256]{1,0:T(8,128)(2,1)}, u32[]{:S(2)}) copy-start(bf16[8192,256]{1,0:T(8,128)(2,1)} %param.6) | copy-start | bytes 12582916
